TPU v7x, 32 devices: a whole 2x2x4 slice. The times are simulated.
32 devices in a mesh: row: 8 (over y, x, core), col: 4 (over z).
Axes of the slice: x: 2, y: 2, z: 4, core: 2. Of those that a mesh axis runs over, the one named last changes fastest.
Arguments:
- corner: bfloat16 [1024, 1024], P('col'), may hold values from -6 to 6
- edge_up: bfloat16 [1024, 36, 128], P('col', None, 'row'), may hold values from -0.1875 to 0.1875
- edge_left: bfloat16 [1024, 36, 1024], P('row', None, 'col'), may hold values from -0.1875 to 0.1875
- doubled: bfloat16 [1296, 1296], replicated, may hold values from -0.15625 to 0.15625
- panel: bfloat16 [36, 1024, 512], P(None, 'col', 'row'), may hold values from -0.03125 to 0.03125
Outputs:
- corner_slab: bfloat16 [36, 36, 128, 1024], P(None, None, 'row', 'col')
- panel_product: bfloat16 [36, 128, 512], P(None, 'row', 'col')
- gram: float32 [512, 512], P('row', 'col')
All inputs are finite; a program needn't handle non-finite values.
Results may differ from a plain program's by a relative error of at most 0.009.
Values may be sent and summed in bfloat16 or wider, within the bound.
A program may use at most 256 MiB of HBM per device.

v0:
```python
import jax
import jax.numpy as jnp
from jax import lax
from jax.sharding import PartitionSpec as P

DL = 36


def contract_site(grown, quad):
    return lax.dot_general(
        quad, grown, (((0, 1), (0, 2)), ((), ())), preferred_element_type=jnp.float32
    ).astype(jnp.bfloat16)


def local(corner, edge_up, edge_left, doubled, panel):
    quad = doubled.reshape(DL, DL, DL, DL)
    alpha_local = edge_up.shape[2]
    partials = lax.dot_general(
        edge_up, corner, (((0,), (0,)), ((), ())), preferred_element_type=jnp.float32
    )
    corner_edge = lax.psum(partials, "col").astype(jnp.bfloat16)
    grown = lax.dot_general(
        corner_edge,
        lax.all_gather(edge_left, "row", axis=0, tiled=True),
        (((2,), (0,)), ((), ())),
        preferred_element_type=jnp.float32,
    ).astype(jnp.bfloat16)
    slab = contract_site(grown, quad)
    partial_product = lax.dot_general(
        slab,
        lax.all_gather(panel, "row", axis=2, tiled=True),
        (((1, 3), (0, 1)), ((), ())),
        preferred_element_type=jnp.float32,
    )
    own_cols = lax.psum_scatter(partial_product, "col", scatter_dimension=2, tiled=True).astype(
        jnp.bfloat16
    )
    rows_all = lax.all_gather(own_cols, "col", axis=2, tiled=True)
    total_rows = DL * alpha_local * lax.axis_size("row")
    gram = lax.psum_scatter(
        (
            lax.dot_general(
                rows_all, own_cols, (((0, 1), (0, 1)), ((), ())), preferred_element_type=jnp.float32
            )
            / total_rows
        ).astype(jnp.bfloat16),
        "row",
        scatter_dimension=0,
        tiled=True,
    ).astype(jnp.float32)
    return (slab, own_cols, gram)


def solution(mesh):
    in_specs = (
        P("col", None),
        P("col", None, "row"),
        P("row", None, "col"),
        P(),
        P(None, "col", "row"),
    )
    out_specs = (P(None, None, "row", "col"), P(None, "row", "col"), P("row", "col"))
    return jax.shard_map(local, mesh=mesh, in_specs=in_specs, out_specs=out_specs, check_vma=False)
```

profile of v0, /device:TPU:25, one launch (start us, length us, event | category | flops | bytes accessed | tf_op | source)
XLA Modules:
  0.0 282.4 jit_solution(14259493160074850872)
XLA Ops:
  7.2 0.0 copy-start
  7.2 0.0 all-gather.3.cloned.1.call-start
  7.2 0.7 all-gather.3.cloned.1.call-update
  7.9 0.0 all-gather.5.cloned.1.call-start
  8.0 0.7 all-gather.5.cloned.1.call-update
  8.7 0.0 reduce-scatter.3.cloned.1.call-start
  8.7 16.5 %reshape.9 = bf16[36,36,36,36]{3,2,1,0:T(8,128)(2,1)} reshape(bf16[1296,1296]{1,0:T(8,128)(2,1)} %param.8) | data formatting | bytes 6718464 | tf_op jit(solution)/shard_map/reshape | solution.py:16
  25.2 0.0 copy-start.3
  25.2 19.9 %copy.8 = bf16[36,36,36,36]{1,3,0,2:T(8,128)(2,1)} copy(bf16[36,36,36,36]{3,2,1,0:T(8,128)(2,1)} %reshape.9) | data formatting | bytes 6718464 | tf_op jit(solution)/shard_map/reshape | solution.py:16
  45.1 0.0 copy-done
  45.1 0.0 copy-done.3
  45.1 0.5 fusion.20
  45.6 82.0 %all-reduce.1 = bf16[36,16,1024]{2,1,0:T(8,128)(2,1)} all-reduce(f32[36,16,1024]{2,1,0:T(8,128)S(1)} %fusion.20), channel_id=1, replica_groups=mesh['row'=8,'col'=4] {'col'}, use_global_device_ids=true, to_apply=%region_0.0 | all-reduce | flops 589824 | bytes 3538944 | tf_op jit(solution)/shard_map/psum | solution.py:21
  127.6 0.0 all-gather.3.cloned.1.call-done
  127.6 17.7 %fusion = bf16[36,16,36,256]{3,1,2,0:T(8,128)(2,1)} fusion(bf16[1024,36,256]{2,0,1:T(8,128)(2,1)} %all-gather.3.cloned.1.call-done, bf16[36,16,1024]{2,1,0:T(8,128)(2,1)} %all-reduce.1), kind=kOutput, calls=%fused_computation.2 | convolution fusion | flops 10871635968 | bytes 30670848 | tf_op jit(solution)/shard_map/dot_general | solution.py:22
  145.3 26.9 %fusion.6 = bf16[36,36,16,256]{3,1,0,2:T(8,128)(2,1)S(1)} fusion(bf16[36,36,36,36]{1,3,0,2:T(8,128)(2,1)} %copy.8, bf16[36,16,36,256]{3,1,2,0:T(8,128)(2,1)} %fusion), kind=kOutput, calls=%fused_computation.7 | convolution fusion | flops 13764722688 | bytes 24592896 | tf_op jit(solution)/shard_map/dot_general | solution.py:10
  172.2 7.7 %copy.12 = bf16[36,36,16,256]{3,2,1,0:T(8,128)(2,1)} copy(bf16[36,36,16,256]{3,1,0,2:T(8,128)(2,1)S(1)} %fusion.6) | data formatting | bytes 21233664
  179.9 0.0 all-gather.5.cloned.1.call-done
  179.9 0.0 copy-start.1
  179.9 12.3 %fusion.13 = f32[36,16,512]{2,1,0:T(8,128)} fusion(bf16[36,36,16,256]{3,2,1,0:T(8,128)(2,1)} %copy.12, bf16[36,256,512]{1,2,0:T(8,128)(2,1)} %all-gather.5.cloned.1.call-done), kind=kOutput, calls=%fused_computation.10 | convolution fusion | flops 5435817984 | bytes 21233664 | tf_op jit(solution)/shard_map/dot_general | solution.py:29
  192.2 0.0 reduce-scatter.3.cloned.1.call-update
  192.2 0.0 reduce-scatter.5.cloned.1.call-start
  192.3 30.3 %reduce-scatter.3.cloned.1.call-done = f32[36,16,128]{2,1,0:T(8,128)} async-done(((f32[36,16,512]{2,1,0:T(8,128)}), f32[36,16,128]{2,1,0:T(8,128)}) %reduce-scatter.3.cloned.1.call-update) | async-done | bytes 294928 | tf_op jit(solution)/shard_map/reduce_scatter | solution.py:35
  222.6 1.0 convert_element_type.25
  223.6 0.0 copy-start.2
  223.6 13.6 %all_gather.11 = bf16[36,16,512]{2,1,0:T(8,128)(2,1)S(1)} all-gather(bf16[36,16,128]{2,1,0:T(8,128)(2,1)S(1)} %convert_element_type.25), channel_id=1, replica_groups=mesh['row'=8,'col'=4] {'col'}, dimensions={2}, use_global_device_ids=true | all-gather | bytes 737280 | tf_op jit(solution)/shard_map/all_gather | solution.py:38
  237.3 1.0 fusion.19
  238.3 0.0 reduce-scatter.5.cloned.1.call-update
  238.3 36.2 %reduce-scatter.5.cloned.1.call-done = bf16[64,128]{1,0:T(8,128)(2,1)} async-done(((bf16[512,128]{1,0:T(8,128)(2,1)}), bf16[64,128]{1,0:T(8,128)(2,1)}) %reduce-scatter.5.cloned.1.call-update) | async-done | bytes 16400 | tf_op jit(solution)/shard_map/reduce_scatter | solution.py:40
  274.5 1.3 convert_element_type.27
  275.9 0.0 copy-done.2
  275.9 0.0 copy-done.1
Async XLA Ops:
  7.2 37.9 %copy-start = (bf16[256,1024]{1,0:T(8,128)(2,1)S(1)}, bf16[256,1024]{1,0:T(8,128)(2,1)}, u32[]{:S(2)}) copy-start(bf16[256,1024]{1,0:T(8,128)(2,1)} %param.5) | copy-start | bytes 1572868
  7.2 120.4 %all-gather.3.cloned.1.call-start = ((), (), s32[]{:S(2)}) async-start(), calls=%async_computation.2 | async-start | bytes 21233664 | tf_op jit(solution)/shard_map/all_gather | solution.py:24
  7.9 172.0 %all-gather.5.cloned.1.call-start = ((), (), s32[]{:S(2)}) async-start(), calls=%async_computation.3 | async-start | bytes 10616832 | tf_op jit(solution)/shard_map/all_gather | solution.py:31
  8.7 213.9 %reduce-scatter.3.cloned.1.call-start = ((), (), s32[]{:S(2)}) async-start(), calls=%async_computation.4 | async-start | bytes 1474560 | tf_op jit(solution)/shard_map/reduce_scatter | solution.py:35
  25.2 19.9 %copy-start.3 = (bf16[256,36,16]{0,2,1:T(8,128)(2,1)S(1)}, bf16[256,36,16]{0,2,1:T(8,128)(2,1)}, u32[]{:S(2)}) copy-start(bf16[256,36,16]{0,2,1:T(8,128)(2,1)} %param.6) | copy-start | bytes 884740
  179.9 96.0 %copy-start.1 = (bf16[256,1024]{1,0:T(8,128)(2,1)S(1)}, bf16[256,1024]{1,0:T(8,128)(2,1)}, u32[]{:S(2)}) copy-start(bf16[256,1024]{1,0:T(8,128)(2,1)} %param.5) | copy-start | bytes 1572868
  192.2 82.3 %reduce-scatter.5.cloned.1.call-start = ((), (), s32[]{:S(2)}) async-start(), calls=%async_computation.5 | async-start | bytes 147456 | tf_op jit(solution)/shard_map/reduce_scatter | solution.py:40
  223.6 52.3 %copy-start.2 = (bf16[36,16,128]{2,1,0:T(8,128)(2,1)}, bf16[36,16,128]{2,1,0:T(8,128)(2,1)S(1)}, u32[]{:S(2)}) copy-start(bf16[36,16,128]{2,1,0:T(8,128)(2,1)S(1)} %convert_element_type.25) | copy-start | bytes 442372
Sparse Core Ops, SparseCore 0:
  9.9 100.1 all-gather.2
  112.0 58.8 all-gather.4
  192.3 30.2 reduce-scatter.2
  238.4 36.0 reduce-scatter.4
where the time goes:
time: 286 us; the launch traced here: 282 us
  blocking collectives  95.7 us (33%)
  waiting for transfers between devices  68 us (24%)
  matrix products  58.4 us (20%)
  local copies, waits for them, and re-layouts  44.1 us (15%)
  between operations  13.8 us (5%)
    psum x1, blocking collectives, local(): corner_edge = lax.psum(partials, 'col').astype(jnp.bfloat16)  82 us
    reshape x2, local copies, waits for them, and re-layouts, local(): quad = doubled.reshape(DL, DL, DL, DL)  36.4 us
    reduce_scatter x1, waiting for transfers between devices, local(): lax.psum_scatter((lax.dot_general(rows_all, own_cols, (((0, 1), (0, 1)),...  36.2 us
    reduce_scatter x1, waiting for transfers between devices, local(): lax.psum_scatter(partial_product, 'col', scatter_dimension=2, tiled=True)  30.3 us
    dot_general x1, matrix products, contract_site(): lax.dot_general(quad, grown, (((0, 1), (0, 2)), ((), ())), preferred_elem...  26.9 us
    dot_general x1, matrix products, local(): lax.dot_general(corner_edge, lax.all_gather(edge_left, 'row', axis=0, til...  17.7 us
    all_gather x1, blocking collectives, local(): rows_all = lax.all_gather(own_cols, 'col', axis=2, tiled=True)  13.6 us
    dot_general x1, matrix products, local(): lax.dot_general(slab, lax.all_gather(panel, 'row', axis=2, tiled=True), (...  12.3 us
  transfers between devices with their start and end apart: 4, of which 2 were waited for; matrix products, arithmetic and copies ran while one was open for 32% of the time, Pallas kernels for 0%

commit v1 on v0

v1 whole, which is shorter than its diff:
```python
import jax
import jax.numpy as jnp
from jax import lax
from jax.experimental import pallas as pl
from jax.experimental.pallas import tpu as pltpu
from jax.sharding import PartitionSpec as P

BF = jnp.bfloat16
F32 = jnp.float32
MESH = pl.DeviceIdType.MESH
CHUNKS = 6


def remote(src, dst, send_sem, recv_sem, device):
    return pltpu.make_async_remote_copy(
        src_ref=src,
        dst_ref=dst,
        send_sem=send_sem,
        recv_sem=recv_sem,
        device_id=device,
        device_id_type=MESH,
    )


def enter(devices):
    barrier = pltpu.get_barrier_semaphore()
    for device in devices:
        pl.semaphore_signal(barrier, inc=1, device_id=device, device_id_type=MESH)
    pl.semaphore_wait(barrier, len(devices))


def grow_kernel(up, corner, left, out, every, grown, parts, sent, got, edge, sends, recvs, zs, zr, local_sem, out_sems):
    dl, delta, beta = left.shape
    dk = parts.shape[1] // 16
    step = dl // CHUNKS
    half = step // 2
    r, c = lax.axis_index("row"), lax.axis_index("col")
    core, x, y = r % 2, (r // 2) % 2, r // 4
    r_core, r_x, r_y = r + 1 - 2 * core, r + 2 - 4 * x, r + 4 - 8 * y
    r_xy = r_x + 4 - 8 * y
    to_core, to_x, to_y = (r_core, c), (r_x, c), (r_y, c)
    z = [(c + d) % 4 for d in (1, 2, 3)]
    enter([to_core, to_x, to_y] + [(r, p) for p in z])

    own = pltpu.make_async_copy(left, every.at[:, pl.ds(r * delta, delta), :], local_sem)
    own.start()

    def block(n, owner, lo, size):
        return every.at[pl.ds(n * step + lo, size), pl.ds(owner * delta, delta), :]

    def move(kind, n, owner, lo, size, device):
        ref = block(n, owner, lo, size)
        return remote(ref, ref, sends.at[kind, n], recvs.at[kind, n], device)

    def first(n):
        src = left.at[pl.ds(n * step, step)]
        dst = block(n, r, 0, step)
        for kind, device in ((0, to_x), (1, to_y), (2, to_core)):
            remote(src, dst, sends.at[kind, n], recvs.at[kind, n], device).start()

    def arrived(kind, n, owner, lo, size):
        move(kind, n, owner, lo, size, to_core).wait_recv()

    first(0)
    first(1)
    for p in range(4):
        parts[p] = jnp.dot(
            up[...], corner[:, p * 256 : (p + 1) * 256], preferred_element_type=F32
        )
        sent[p] = parts[p].astype(BF)
    z_out = [remote(sent.at[z[d]], got.at[d], zs.at[0, d], zr.at[0, d], (r, z[d])) for d in range(3)]
    for copy in z_out:
        copy.start()
    z_all = [remote(edge.at[c], edge.at[c], zs.at[1, d], zr.at[1, d], (r, z[d])) for d in range(3)]

    own.wait()

    def grow(n):
        @pl.loop(n * step, (n + 1) * step)
        def _(l):
            acc = jnp.dot(edge[0], every[l, 0:256, :], preferred_element_type=F32)
            for p in range(1, 4):
                acc += jnp.dot(
                    edge[p], every[l, p * 256 : (p + 1) * 256, :], preferred_element_type=F32
                )
            grown[:, l] = acc.astype(BF).reshape(dk, 16, beta)

        pltpu.make_async_copy(
            grown.at[:, pl.ds(n * step, step)], out.at[:, pl.ds(n * step, step)], out_sems.at[n]
        ).start()

    done = 0
    for s in range(CHUNKS + 2):
        if s + 2 < CHUNKS:
            first(s + 2)
        if s < CHUNKS:
            arrived(0, s, r_x, 0, step)
            move(4, s, r_x, half, half, to_y).start()
            move(5, s, r_x, 0, step, to_core).start()
            arrived(1, s, r_y, 0, step)
            move(3, s, r_y, 0, half, to_x).start()
            move(6, s, r_y, 0, step, to_core).start()
        if 1 <= s <= CHUNKS:
            arrived(3, s - 1, r_xy, 0, half)
            move(7, s - 1, r_xy, 0, half, to_core).start()
            arrived(4, s - 1, r_xy, half, half)
            move(8, s - 1, r_xy, half, half, to_core).start()
        if s == 2:
            for d in range(3):
                z_out[d].wait_recv()
            edge[c] = (
                parts[c] + got[0].astype(F32) + got[1].astype(F32) + got[2].astype(F32)
            ).astype(BF)
            for copy in z_all:
                copy.start()
        if s == 4:
            for copy in z_all:
                copy.wait_recv()
        if s >= 4:
            while done <= s - 2:
                for kind, lo, size in ((2, 0, step), (5, 0, step), (6, 0, step), (7, 0, half), (8, half, half)):
                    arrived(kind, done, r_core, lo, size)
                grow(done)
                done += 1
    for n in range(CHUNKS):
        for kind, size in enumerate((step, step, step, half, half, step, step, half, half)):
            move(kind, n, r, 0, size, to_core).wait_send()
        pltpu.make_async_copy(
            grown.at[:, pl.ds(n * step, step)], out.at[:, pl.ds(n * step, step)], out_sems.at[n]
        ).wait()
    for copy in z_out + z_all:
        copy.wait_send()


def grow(edge_up, corner, edge_left):
    gamma, dk, alpha = edge_up.shape
    delta, dl, beta = edge_left.shape
    rows = dk * alpha
    vmem, any_space = pl.BlockSpec(memory_space=pltpu.VMEM), pl.BlockSpec(memory_space=pl.ANY)
    dma = pltpu.SemaphoreType.DMA
    return pl.pallas_call(
        grow_kernel,
        out_shape=jax.ShapeDtypeStruct((dk, dl, alpha, beta), BF),
        in_specs=[vmem, vmem, any_space],
        out_specs=any_space,
        scratch_shapes=[
            pltpu.VMEM((dl, 8 * delta, beta), BF),
            pltpu.VMEM((dk, dl, alpha, beta), BF),
            pltpu.VMEM((4, rows, 256), F32),
            pltpu.VMEM((4, rows, 256), BF),
            pltpu.VMEM((3, rows, 256), BF),
            pltpu.VMEM((4, rows, 256), BF),
            dma((9, CHUNKS)),
            dma((9, CHUNKS)),
            dma((2, 3)),
            dma((2, 3)),
            dma,
            dma((CHUNKS,)),
        ],
        compiler_params=pltpu.CompilerParams(
            collective_id=0, has_side_effects=True, vmem_limit_bytes=52 * 2**20
        ),
        name="grow",
    )(edge_up.transpose(1, 2, 0).reshape(rows, gamma), corner, edge_left.transpose(1, 0, 2))


def finish_kernel(total_rows, partial, cols, gram, sent, got, wide, tiles, landed, zs, zr, rs, rr):
    r, c = lax.axis_index("row"), lax.axis_index("col")
    z = [(c + d) % 4 for d in (1, 2, 3)]
    others = [(r + d) % 8 for d in range(1, 8)]
    enter([(r, p) for p in z] + [(p, c) for p in others])
    for p in range(4):
        sent[p] = partial[:, p * 128 : (p + 1) * 128].astype(BF)
    out = [remote(sent.at[z[d]], got.at[d], zs.at[0, d], zr.at[0, d], (r, z[d])) for d in range(3)]
    for copy in out:
        copy.start()
    mine = partial[:, pl.ds(pl.multiple_of(c * 128, 128), 128)]
    for d in range(3):
        out[d].wait_recv()
        mine += got[d].astype(F32)
    mine = mine.astype(BF)
    wide[c] = mine
    cols[...] = mine
    back = [remote(wide.at[c], wide.at[c], zs.at[1, d], zr.at[1, d], (r, z[d])) for d in range(3)]
    for copy in back:
        copy.start()
    for copy in back:
        copy.wait_recv()
    for p in range(4):
        prod = lax.dot_general(
            wide[p], mine, (((0,), (0,)), ((), ())), preferred_element_type=F32
        ) / total_rows
        tiles[2 * p] = prod[:64].astype(BF)
        tiles[2 * p + 1] = prod[64:].astype(BF)
    spread = [
        remote(tiles.at[others[d]], landed.at[d], rs.at[d], rr.at[d], (others[d], c))
        for d in range(7)
    ]
    for copy in spread:
        copy.start()
    total = tiles[r].astype(F32)
    for d in range(7):
        spread[d].wait_recv()
        total += landed[d].astype(F32)
    gram[...] = total
    for copy in out + back + spread:
        copy.wait_send()


def finish(partial, total_rows):
    rows = partial.shape[0]
    vmem = pl.BlockSpec(memory_space=pltpu.VMEM)
    dma = pltpu.SemaphoreType.DMA

    def body(*refs):
        finish_kernel(total_rows, *refs)

    return pl.pallas_call(
        body,
        out_shape=(
            jax.ShapeDtypeStruct((rows, 128), BF),
            jax.ShapeDtypeStruct((64, 128), F32),
        ),
        in_specs=[vmem],
        out_specs=(vmem, vmem),
        scratch_shapes=[
            pltpu.VMEM((4, rows, 128), BF),
            pltpu.VMEM((3, rows, 128), BF),
            pltpu.VMEM((4, rows, 128), BF),
            pltpu.VMEM((8, 64, 128), BF),
            pltpu.VMEM((7, 64, 128), BF),
            dma((2, 3)),
            dma((2, 3)),
            dma((7,)),
            dma((7,)),
        ],
        compiler_params=pltpu.CompilerParams(
            collective_id=1, has_side_effects=True, vmem_limit_bytes=16 * 2**20
        ),
        name="finish",
    )(partial)


def general(corner, edge_up, edge_left, doubled, panel):
    dl, alpha_local = edge_up.shape[1], edge_up.shape[2]
    quad = doubled.reshape(dl, dl, dl, dl)
    partials = lax.dot_general(
        edge_up, corner, (((0,), (0,)), ((), ())), preferred_element_type=F32
    )
    corner_edge = lax.psum(partials, "col").astype(BF)
    grown = lax.dot_general(
        corner_edge,
        lax.all_gather(edge_left, "row", axis=0, tiled=True),
        (((2,), (0,)), ((), ())),
        preferred_element_type=F32,
    ).astype(BF)
    slab = lax.dot_general(
        quad, grown, (((0, 1), (0, 2)), ((), ())), preferred_element_type=F32
    ).astype(BF)
    partial_product = lax.dot_general(
        slab,
        lax.all_gather(panel, "row", axis=2, tiled=True),
        (((1, 3), (0, 1)), ((), ())),
        preferred_element_type=F32,
    )
    own_cols = lax.psum_scatter(partial_product, "col", scatter_dimension=2, tiled=True).astype(BF)
    rows_all = lax.all_gather(own_cols, "col", axis=2, tiled=True)
    total_rows = dl * alpha_local * lax.axis_size("row")
    gram = lax.psum_scatter(
        (
            lax.dot_general(
                rows_all, own_cols, (((0, 1), (0, 1)), ((), ())), preferred_element_type=F32
            )
            / total_rows
        ).astype(BF),
        "row",
        scatter_dimension=0,
        tiled=True,
    ).astype(F32)
    return (slab, own_cols, gram)


def local(corner, edge_up, edge_left, doubled, panel):
    n_row, n_col = lax.axis_size("row"), lax.axis_size("col")
    if (n_row, n_col) != (8, 4):
        return general(corner, edge_up, edge_left, doubled, panel)
    dl, alpha = edge_up.shape[1], edge_up.shape[2]
    beta = edge_left.shape[2]
    grown = grow(edge_up, corner, edge_left)
    grown, panel = lax.optimization_barrier((grown, panel))
    wide = lax.all_gather(panel, "row", axis=2, tiled=True)
    slab = (
        lax.dot_general(
            doubled,
            grown.reshape(dl * dl, alpha, beta),
            (((0,), (0,)), ((), ())),
            preferred_element_type=F32,
        )
        .astype(BF)
        .reshape(dl, dl, alpha, beta)
    )
    partial = lax.dot_general(
        slab, wide, (((1, 3), (0, 1)), ((), ())), preferred_element_type=F32
    ).reshape(dl * alpha, -1)
    cols, gram = finish(partial, dl * alpha * n_row)
    return (slab, cols.reshape(dl, alpha, -1), gram)


def solution(mesh):
    in_specs = (
        P("col", None),
        P("col", None, "row"),
        P("row", None, "col"),
        P(),
        P(None, "col", "row"),
    )
    out_specs = (P(None, None, "row", "col"), P(None, "row", "col"), P("row", "col"))
    return jax.shard_map(local, mesh=mesh, in_specs=in_specs, out_specs=out_specs, check_vma=False)
```

time: 286 us -> 217 us (0.76); the launches traced: 282 us -> 216 us
  Pallas kernels: 0 us -> 128 us
  blocking collectives: 95.7 us -> 0 us
  waiting for transfers between devices: 68 us -> 10.7 us
  matrix products: 58.4 us -> 34.2 us
  local copies, waits for them, and re-layouts: 44.1 us -> 29.9 us
    pallas_call x0 -> x2, Pallas kernels: none -> 128 us  [the longest x1 93.4 us: grow(): pl.pallas_call(grow_kernel, out_shape=jax.ShapeDtypeStruct((dk, dl, alpha...]
    psum x1 -> x0, blocking collectives: 82 us -> none  [local(): corner_edge = lax.psum(partials, 'col').astype(jnp.bfloat16)]
    reduce_scatter x2 -> x0, waiting for transfers between devices: 66.6 us -> none  [the longest x1 36.2 us: local(): lax.psum_scatter((lax.dot_general(rows_all, own_cols, (((0, 1), (0, 1)),...]
    reshape x2 -> x0, local copies, waits for them, and re-layouts: 36.4 us -> none  [local(): quad = doubled.reshape(DL, DL, DL, DL)]
    dot_general x5 -> x2, matrix products: 58.4 us -> 34.2 us  [the longest x1 23.1 us: local(): lax.dot_general(doubled, grown.reshape(dl * dl, alpha, beta), (((0,), (0,...]
    convert_element_type x0 -> x1, local copies, waits for them, and re-layouts: none -> 17.8 us  [local(): slab = lax.dot_general(doubled, grown.reshape(dl * dl, alpha, beta), (((0...]
    all_gather x1 -> x0, blocking collectives: 13.6 us -> none  [local(): rows_all = lax.all_gather(own_cols, 'col', axis=2, tiled=True)]
    all_gather x2 -> x1, waiting for transfers between devices: 0.01 us -> 10.6 us  [local(): wide = lax.all_gather(panel, 'row', axis=2, tiled=True)]
  transfers between devices with their start and end apart: 4 -> 1, of which waited for: 2 -> 1; matrix products, arithmetic and copies ran while one was open for 32% -> 21% of each run, Pallas kernels for 0% -> 0%
where the time goes in v1:
time: 217 us; the launch traced here: 216 us
  Pallas kernels  128 us (59%)
  matrix products  34.2 us (16%)
  local copies, waits for them, and re-layouts  29.9 us (14%)
  between operations  14.1 us (6%)
  waiting for transfers between devices  10.7 us (5%)
    pallas_call x1, Pallas kernels, grow(): pl.pallas_call(grow_kernel, out_shape=jax.ShapeDtypeStruct((dk, dl, alpha...  93.4 us
    pallas_call x1, Pallas kernels, finish(): pl.pallas_call(body, out_shape=(jax.ShapeDtypeStruct((rows, 128), BF), ja...  34.2 us
    dot_general x1, matrix products, local(): lax.dot_general(doubled, grown.reshape(dl * dl, alpha, beta), (((0,), (0,...  23.1 us
    convert_element_type x1, local copies, waits for them, and re-layouts, local(): slab = lax.dot_general(doubled, grown.reshape(dl * dl, alpha, beta), (((0...  17.8 us
    dot_general x1, matrix products, local(): lax.dot_general(slab, wide, (((1, 3), (0, 1)), ((), ())), preferred_eleme...  11.2 us
    all_gather x1, waiting for transfers between devices, local(): wide = lax.all_gather(panel, 'row', axis=2, tiled=True)  10.6 us
    unnamed x8, local copies, waits for them, and re-layouts  7.4 us
    dot_general x1, local copies, waits for them, and re-layouts, local(): lax.dot_general(slab, wide, (((1, 3), (0, 1)), ((), ())), preferred_eleme...  4.74 us
  transfers between devices with their start and end apart: 1, of which 1 were waited for; matrix products, arithmetic and copies ran while one was open for 21% of the time, Pallas kernels for 0%

profile of v1, /device:TPU:25, one launch (start us, length us, event | category | flops | bytes accessed | tf_op | source)
XLA Modules:
  0.0 216.5 jit_solution(17474776977800258280)
XLA Ops:
  7.2 0.0 all-gather.2.cloned.1.call-start
  7.2 0.0 copy-start
  7.2 1.0 copy-done
  8.3 0.0 copy-start.1
  8.3 1.0 copy-done.1
  9.2 93.4 %grow.1 = bf16[36,36,16,256]{3,2,1,0:T(8,128)(2,1)} custom-call(bf16[576,256]{1,0:T(8,128)(2,1)S(1)} %bitcast.19, bf16[256,1024]{1,0:T(8,128)(2,1)S(1)} %copy-done, bf16[36,128,256]{2,1,0:T(8,128)(2,1)} %bitcast.25), custom_call_target="tpu_custom_call" | custom-call | tf_op jit(solution)/shard_map/grow/pallas_call | solution.py:141
  102.6 0.0 all-gather.2.cloned.1.call-update
  102.6 23.1 %fusion = bf16[1296,16,256]{2,0,1:T(8,128)(2,1)} fusion(bf16[1296,16,256]{2,1,0:T(8,128)(2,1)} %bitcast.23, bf16[1296,1296]{1,0:T(8,128)(2,1)} %param.8), kind=kOutput, calls=%fused_computation.1 | convolution fusion | flops 13764722688 | bytes 24592896 | tf_op jit(solution)/shard_map/dot_general | solution.py:293
  125.7 17.8 %copy.17 = bf16[1296,16,256]{2,1,0:T(8,128)(2,1)S(1)} copy(bf16[1296,16,256]{2,0,1:T(8,128)(2,1)} %fusion) | data formatting | bytes 21233664 | tf_op jit(solution)/shard_map/convert_element_type | solution.py:299
  143.5 0.0 copy-start.2
  143.5 4.1 %copy-done.2 = bf16[1296,16,256]{2,1,0:T(8,128)(2,1)} copy-done((bf16[1296,16,256]{2,1,0:T(8,128)(2,1)}, bf16[1296,16,256]{2,1,0:T(8,128)(2,1)S(1)}, u32[]{:S(2)}) %copy-start.2) | copy-done | bytes 10616856
  147.6 4.7 %copy.18 = bf16[36,16,36,256]{3,1,0,2:T(8,128)(2,1)} copy(bf16[36,16,36,256]{3,1,2,0:T(8,128)(2,1)S(1)} %bitcast.21) | data formatting | bytes 21233664 | tf_op jit(solution)/shard_map/dot_general | solution.py:302
  152.3 10.6 %all-gather.2.cloned.1.call-done = bf16[36,256,512]{1,2,0:T(8,128)(2,1)} async-done(((bf16[36,256,64]{1,2,0:T(8,128)(2,1)}), bf16[36,256,512]{1,2,0:T(8,128)(2,1)}) %all-gather.2.cloned.1.call-update) | async-done | bytes 9437200 | tf_op jit(solution)/shard_map/all_gather | solution.py:291
  163.0 11.2 %convolution_bitcast_fusion.refs_0_ = f32[576,512]{1,0:T(8,128)S(1)} fusion(bf16[576,36,256]{2,0,1:T(8,128)(2,1)} %bitcast.24, bf16[36,256,512]{1,2,0:T(8,128)(2,1)} %all-gather.2.cloned.1.call-done), kind=kOutput, calls=%fused_computation.4 | convolution fusion | flops 5435817984 | bytes 21233664 | tf_op jit(solution)/shard_map/dot_general | solution.py:302
  174.1 34.2 %finish.1 = (bf16[576,128]{1,0:T(8,128)(2,1)S(1)}, f32[64,128]{1,0:T(8,128)S(1)}) custom-call(f32[576,512]{1,0:T(8,128)S(1)} %convolution_bitcast_fusion.refs_0_), custom_call_target="tpu_custom_call" | custom-call | tf_op jit(solution)/shard_map/finish/pallas_call | solution.py:218
  208.3 0.7 copy.25
  209.0 0.6 copy.26
Async XLA Ops:
  7.2 155.8 %all-gather.2.cloned.1.call-start = ((), (), s32[]{:S(2)}) async-start(), calls=%async_computation | async-start | bytes 10616832 | tf_op jit(solution)/shard_map/all_gather | solution.py:291
  7.2 1.0 copy-start
  8.3 1.0 copy-start.1
  143.5 4.1 %copy-start.2 = (bf16[1296,16,256]{2,1,0:T(8,128)(2,1)}, bf16[1296,16,256]{2,1,0:T(8,128)(2,1)S(1)}, u32[]{:S(2)}) copy-start(bf16[1296,16,256]{2,1,0:T(8,128)(2,1)S(1)} %copy.17) | copy-start | bytes 31850500
Sparse Core Ops, SparseCore 0:
  102.7 60.2 all-gather.1

commit v2 on v1

--- a/solution.py
+++ b/solution.py
@@ -61,8 +61,8 @@
     def arrived(kind, n, owner, lo, size):
         move(kind, n, owner, lo, size, to_core).wait_recv()
 
-    first(0)
-    first(1)
+    for n in range(6):
+        first(n)
     for p in range(4):
         parts[p] = jnp.dot(
             up[...], corner[:, p * 256 : (p + 1) * 256], preferred_element_type=F32
@@ -91,8 +91,8 @@
 
     done = 0
     for s in range(CHUNKS + 2):
-        if s + 2 < CHUNKS:
-            first(s + 2)
+        if s + 6 < CHUNKS:
+            first(s + 6)
         if s < CHUNKS:
             arrived(0, s, r_x, 0, step)
             move(4, s, r_x, half, half, to_y).start()
@@ -113,10 +113,10 @@
             ).astype(BF)
             for copy in z_all:
                 copy.start()
-        if s == 4:
+        if s == 5:
             for copy in z_all:
                 copy.wait_recv()
-        if s >= 4:
+        if s >= 5:
             while done <= s - 2:
                 for kind, lo, size in ((2, 0, step), (5, 0, step), (6, 0, step), (7, 0, half), (8, half, half)):
                     arrived(kind, done, r_core, lo, size)

time: 217 us -> 231 us (1.065)
  Pallas kernels: 128 us -> 142 us
    pallas_call x1, Pallas kernels: 93.4 us -> 108 us  [grow(): pl.pallas_call(grow_kernel, out_shape=jax.ShapeDtypeStruct((dk, dl, alpha...]
  transfers between devices with their start and end apart: 1 -> 1, of which waited for: 1 -> 1; matrix products, arithmetic and copies ran while one was open for 21% -> 20% of each run, Pallas kernels for 0% -> 0%
where the time goes in v2:
time: 231 us
  Pallas kernels  142 us (61%)
  matrix products  34.2 us (15%)
  local copies, waits for them, and re-layouts  29.9 us (13%)
  between operations  14.1 us (6%)
  waiting for transfers between devices  10.7 us (5%)
    pallas_call x1, Pallas kernels, grow(): pl.pallas_call(grow_kernel, out_shape=jax.ShapeDtypeStruct((dk, dl, alpha...  108 us
    pallas_call x1, Pallas kernels, finish(): pl.pallas_call(body, out_shape=(jax.ShapeDtypeStruct((rows, 128), BF), ja...  34.2 us
    dot_general x1, matrix products, local(): lax.dot_general(doubled, grown.reshape(dl * dl, alpha, beta), (((0,), (0,...  23.1 us
    convert_element_type x1, local copies, waits for them, and re-layouts, local(): slab = lax.dot_general(doubled, grown.reshape(dl * dl, alpha, beta), (((0...  17.8 us
    dot_general x1, matrix products, local(): lax.dot_general(slab, wide, (((1, 3), (0, 1)), ((), ())), preferred_eleme...  11.2 us
    all_gather x1, waiting for transfers between devices, local(): wide = lax.all_gather(panel, 'row', axis=2, tiled=True)  10.7 us
    unnamed x8, local copies, waits for them, and re-layouts  7.4 us
    dot_general x1, local copies, waits for them, and re-layouts, local(): lax.dot_general(slab, wide, (((1, 3), (0, 1)), ((), ())), preferred_eleme...  4.74 us
  transfers between devices with their start and end apart: 1, of which 1 were waited for; matrix products, arithmetic and copies ran while one was open for 20% of the time, Pallas kernels for 0%

profile of v2, /device:TPU:25, one launch (start us, length us, event | category | flops | bytes accessed | tf_op | source)
XLA Modules:
  0.0 231.1 jit_solution(11590734671075864174)
XLA Ops:
  7.2 0.0 all-gather.2.cloned.1.call-start
  7.2 0.0 copy-start
  7.2 1.0 copy-done
  8.3 0.0 copy-start.1
  8.3 1.0 copy-done.1
  9.2 107.9 %grow.1 = bf16[36,36,16,256]{3,2,1,0:T(8,128)(2,1)} custom-call(bf16[576,256]{1,0:T(8,128)(2,1)S(1)} %bitcast.19, bf16[256,1024]{1,0:T(8,128)(2,1)S(1)} %copy-done, bf16[36,128,256]{2,1,0:T(8,128)(2,1)} %bitcast.25), custom_call_target="tpu_custom_call" | custom-call | tf_op jit(solution)/shard_map/grow/pallas_call | solution.py:141
  117.1 0.0 all-gather.2.cloned.1.call-update
  117.2 23.1 %fusion = bf16[1296,16,256]{2,0,1:T(8,128)(2,1)} fusion(bf16[1296,16,256]{2,1,0:T(8,128)(2,1)} %bitcast.23, bf16[1296,1296]{1,0:T(8,128)(2,1)} %param.8), kind=kOutput, calls=%fused_computation.1 | convolution fusion | flops 13764722688 | bytes 24592896 | tf_op jit(solution)/shard_map/dot_general | solution.py:293
  140.2 17.8 %copy.17 = bf16[1296,16,256]{2,1,0:T(8,128)(2,1)S(1)} copy(bf16[1296,16,256]{2,0,1:T(8,128)(2,1)} %fusion) | data formatting | bytes 21233664 | tf_op jit(solution)/shard_map/convert_element_type | solution.py:299
  158.0 0.0 copy-start.2
  158.0 4.1 %copy-done.2 = bf16[1296,16,256]{2,1,0:T(8,128)(2,1)} copy-done((bf16[1296,16,256]{2,1,0:T(8,128)(2,1)}, bf16[1296,16,256]{2,1,0:T(8,128)(2,1)S(1)}, u32[]{:S(2)}) %copy-start.2) | copy-done | bytes 10616856
  162.2 4.7 %copy.18 = bf16[36,16,36,256]{3,1,0,2:T(8,128)(2,1)} copy(bf16[36,16,36,256]{3,1,2,0:T(8,128)(2,1)S(1)} %bitcast.21) | data formatting | bytes 21233664 | tf_op jit(solution)/shard_map/dot_general | solution.py:302
  166.9 10.7 %all-gather.2.cloned.1.call-done = bf16[36,256,512]{1,2,0:T(8,128)(2,1)} async-done(((bf16[36,256,64]{1,2,0:T(8,128)(2,1)}), bf16[36,256,512]{1,2,0:T(8,128)(2,1)}) %all-gather.2.cloned.1.call-update) | async-done | bytes 9437200 | tf_op jit(solution)/shard_map/all_gather | solution.py:291
  177.6 11.2 %convolution_bitcast_fusion.refs_0_ = f32[576,512]{1,0:T(8,128)S(1)} fusion(bf16[576,36,256]{2,0,1:T(8,128)(2,1)} %bitcast.24, bf16[36,256,512]{1,2,0:T(8,128)(2,1)} %all-gather.2.cloned.1.call-done), kind=kOutput, calls=%fused_computation.4 | convolution fusion | flops 5435817984 | bytes 21233664 | tf_op jit(solution)/shard_map/dot_general | solution.py:302
  188.8 34.2 %finish.1 = (bf16[576,128]{1,0:T(8,128)(2,1)S(1)}, f32[64,128]{1,0:T(8,128)S(1)}) custom-call(f32[576,512]{1,0:T(8,128)S(1)} %convolution_bitcast_fusion.refs_0_), custom_call_target="tpu_custom_call" | custom-call | tf_op jit(solution)/shard_map/finish/pallas_call | solution.py:218
  223.0 0.7 copy.25
  223.6 0.6 copy.26
Async XLA Ops:
  7.2 170.4 %all-gather.2.cloned.1.call-start = ((), (), s32[]{:S(2)}) async-start(), calls=%async_computation | async-start | bytes 10616832 | tf_op jit(solution)/shard_map/all_gather | solution.py:291
  7.2 1.0 copy-start
  8.3 1.0 copy-start.1
  158.0 4.1 %copy-start.2 = (bf16[1296,16,256]{2,1,0:T(8,128)(2,1)}, bf16[1296,16,256]{2,1,0:T(8,128)(2,1)S(1)}, u32[]{:S(2)}) copy-start(bf16[1296,16,256]{2,1,0:T(8,128)(2,1)S(1)} %copy.17) | copy-start | bytes 31850500
Sparse Core Ops, SparseCore 0:
  117.3 60.2 all-gather.1
